TPU v7x, 128 devices: a whole 4x4x4 slice. The times are simulated.
128 devices in a mesh: ctx: 32 (over z, x, core), mp: 4 (over y).
Axes of the slice: x: 4, y: 4, z: 4, core: 2. Of those that a mesh axis runs over, the one named last changes fastest.
Arguments:
- query_one: bfloat16 [4096, 65536], P('mp', 'ctx'), may hold values from -6 to 6
- key_one: bfloat16 [4096, 65536], P('mp', 'ctx'), may hold values from -6 to 6
- value_one: bfloat16 [4096, 65536], P('mp', 'ctx'), may hold values from -6 to 6
- query_two: bfloat16 [4096, 65536], P('mp', 'ctx'), may hold values from -6 to 6
- key_two: bfloat16 [4096, 65536], P('mp', 'ctx'), may hold values from -6 to 6
- conv_weights: float32 [2, 3, 3, 4096], P(None, None, None, 'mp'), may hold values from -3 to 3
- mr_filter: bfloat16 [256, 128], P('mp'), may hold values from -0.5 to 0.5
- li_rate: float32 [256, 16], P('mp'), may hold values from 1.5258789e-07 to 0.08
- li_residue: float32 [256, 16], P('mp'), may hold values from -1.5 to 1.5
- norm_gain: float32 [4096], P('mp'), may hold values from 0.1 to 1.9
Outputs:
- normed: bfloat16 [4096, 65536], P('mp', 'ctx')
All inputs are finite; a program needn't handle non-finite values.
Results may differ from a plain program's by a relative error of at most 0.0075.
Values may be sent and summed in bfloat16 or wider, within the bound.
A program may use at most 192 MiB of HBM per device.

v0:
```python
import jax
import jax.numpy as jnp
from jax import lax
from jax.sharding import PartitionSpec as P

D = 4096
GROUP = 16
LI_BLOCK = 256


def passed_along(block, axis, distance):
    devices = range(lax.axis_size(axis))
    route = [(i - distance, i) for i in devices if i - distance in devices]
    return lax.ppermute(block, axis, route)


def short_filter(extended, weights):
    as_float = extended.astype(jnp.float32)
    return (
        weights[0][:, None] * as_float[:, 2:]
        + weights[1][:, None] * as_float[:, 1:-1]
        + weights[2][:, None] * as_float[:, :-2]
    )


def medium_kernel(taps):
    group_count, tap_count = taps.shape
    pattern = jnp.concatenate(
        [
            jnp.zeros((group_count, 1), taps.dtype),
            jnp.flip(taps, axis=1),
            jnp.zeros((group_count, 2 * tap_count - 1), taps.dtype),
        ],
        axis=1,
    )
    tiled = jnp.tile(pattern, (1, tap_count))[:, : tap_count * (3 * tap_count - 1)]
    skewed = tiled.reshape(group_count, tap_count, 3 * tap_count - 1)[:, :, : 2 * tap_count]
    return jnp.swapaxes(skewed, 1, 2)


def medium_filter(extended, kernel, group_width):
    tap_count = kernel.shape[2]
    chan_count = extended.shape[0]
    out_rows = extended.shape[1] - tap_count
    count_of_groups = chan_count // group_width
    count_of_blocks = out_rows // tap_count
    first_half = extended[:, :out_rows].reshape(
        count_of_groups, group_width * count_of_blocks, tap_count
    )
    second_half = extended[:, tap_count:].reshape(
        count_of_groups, group_width * count_of_blocks, tap_count
    )
    mixed = jnp.einsum(
        "gmk,gki->gmi", first_half, kernel[:, :tap_count], preferred_element_type=jnp.float32
    )
    mixed = mixed + jnp.einsum(
        "gmk,gki->gmi", second_half, kernel[:, tap_count:], preferred_element_type=jnp.float32
    )
    return mixed.reshape(chan_count, out_rows)


def filter_tables(rate, residue, block_size):
    lag_values = jnp.arange(block_size, dtype=jnp.float32)
    amplitude = residue * jnp.sqrt(rate)
    decay = jnp.exp(-rate[:, :, None] * lag_values)
    difference = (
        jnp.arange(block_size, dtype=jnp.int32)[None, :]
        - jnp.arange(block_size, dtype=jnp.int32)[:, None]
    )
    lag_grid = jnp.clip(difference, 0, block_size - 1).astype(jnp.float32)
    toeplitz = jnp.zeros((rate.shape[0], block_size, block_size), jnp.float32)
    for mode_index in range(rate.shape[1]):
        toeplitz = toeplitz + amplitude[:, mode_index, None, None] * jnp.exp(
            -rate[:, mode_index, None, None] * lag_grid[None]
        )
    kernel_block = jnp.where((difference >= 0)[None], toeplitz, jnp.zeros_like(toeplitz)).astype(
        jnp.bfloat16
    )
    input_projection = jnp.flip(decay, axis=2).astype(jnp.bfloat16)
    output_readout = amplitude[:, :, None] * decay * jnp.exp(-rate)[:, :, None]
    stride_decay = jnp.exp(-rate * block_size)
    return (kernel_block, input_projection, output_readout, stride_decay)


def chain_pair(earlier, later):
    return (earlier[0] * later[0], later[0] * earlier[1] + later[1])


def long_filter(values, tables, start_state):
    kernel_block, input_projection, output_readout, stride_decay = tables
    count_of_groups, group_width, row_count = values.shape
    block_size = kernel_block.shape[1]
    count_of_blocks = row_count // block_size
    count_of_modes = input_projection.shape[1]
    sequence_pieces = values.reshape(count_of_groups, group_width * count_of_blocks, block_size)
    within = jnp.einsum(
        "gmj,gji->gmi", sequence_pieces, kernel_block, preferred_element_type=jnp.float32
    )
    local_partial_terms = jnp.einsum(
        "phw,psw->phs", sequence_pieces, input_projection, preferred_element_type=jnp.float32
    )
    local_partial_terms = local_partial_terms.reshape(
        count_of_groups, group_width, count_of_blocks, count_of_modes
    )
    decay_four = stride_decay[:, None, None, :]
    local_partial_terms = jnp.concatenate(
        [
            local_partial_terms[:, :, :1] + decay_four * start_state[:, :, None],
            local_partial_terms[:, :, 1:],
        ],
        axis=2,
    )
    factor = jnp.broadcast_to(decay_four, local_partial_terms.shape)
    _, states = lax.associative_scan(chain_pair, (factor, local_partial_terms), axis=2)
    preceding_rows = jnp.concatenate([start_state[:, :, None], states[:, :, :-1]], axis=2)
    carried_state = jnp.einsum(
        "dkp,dps->dks",
        preceding_rows.reshape(count_of_groups, group_width * count_of_blocks, count_of_modes),
        output_readout,
        precision=lax.Precision.HIGHEST,
    )
    return (
        (within + carried_state).reshape(count_of_groups, group_width, row_count),
        states[:, :, -1],
    )


def per_device(
    query_one,
    key_one,
    value_one,
    query_two,
    key_two,
    conv_weights,
    mr_filter,
    li_rate,
    li_residue,
    norm_gain,
):
    group_width = GROUP
    tap_count = mr_filter.shape[1]
    kernel_taps = medium_kernel(mr_filter)
    edge_cols = jnp.stack(
        [query_one[:, -2:], key_one[:, -2:], value_one[:, -2:], query_two[:, -2:], key_two[:, -2:]],
        axis=0,
    )
    edge_cols = passed_along(edge_cols, "ctx", 1)
    query_conv = short_filter(
        jnp.concatenate([edge_cols[0], query_one], axis=1), conv_weights[0, 0]
    )
    key_conv = short_filter(jnp.concatenate([edge_cols[1], key_one], axis=1), conv_weights[0, 1])
    value_conv = short_filter(
        jnp.concatenate([edge_cols[2], value_one], axis=1), conv_weights[0, 2]
    )
    product = (key_conv * value_conv).astype(jnp.bfloat16)
    rim_cols = passed_along(product[:, -tap_count:], "ctx", 1)
    mixed = medium_filter(jnp.concatenate([rim_cols, product], axis=1), kernel_taps, group_width)
    layer_one = (query_conv * mixed).astype(jnp.bfloat16)
    tail_cols = passed_along(layer_one[:, -2:], "ctx", 1)
    value_input = jnp.concatenate([tail_cols, layer_one], axis=1)
    second_query_rim = edge_cols[3]
    second_key_rim = edge_cols[4]
    query_next = short_filter(
        jnp.concatenate([second_query_rim, query_two], axis=1), conv_weights[1, 0]
    )
    key_next = short_filter(jnp.concatenate([second_key_rim, key_two], axis=1), conv_weights[1, 1])
    value_next = short_filter(value_input, conv_weights[1, 2])
    second = (key_next * value_next).astype(jnp.bfloat16)
    spread = lax.all_to_all(second, "ctx", split_axis=0, concat_axis=1, tiled=True)
    share_count = spread.shape[0] // group_width
    first_group = lax.axis_index("ctx") * share_count
    rate_part = lax.dynamic_slice_in_dim(li_rate, first_group, share_count, 0)
    residue_part = lax.dynamic_slice_in_dim(li_residue, first_group, share_count, 0)
    tables = filter_tables(rate_part, residue_part, LI_BLOCK)
    seq_rows = spread.shape[1]
    start_state = jnp.zeros((share_count, group_width, rate_part.shape[1]), jnp.float32)
    full_result, _ = long_filter(
        spread.reshape(share_count, group_width, seq_rows), tables, start_state
    )
    share_result = full_result.reshape(share_count * group_width, seq_rows).astype(jnp.bfloat16)
    filtered = lax.all_to_all(share_result, "ctx", split_axis=1, concat_axis=0, tiled=True)
    gated = query_next * filtered.astype(jnp.float32)
    col_squares = jnp.sum(gated * gated, axis=0)
    total = lax.psum(col_squares, "mp")
    scale = lax.rsqrt(total / D + 1e-05)
    return (gated * scale[None, :] * norm_gain[:, None]).astype(jnp.bfloat16)


def solution(mesh):
    in_specs = (
        P("mp", "ctx"),
        P("mp", "ctx"),
        P("mp", "ctx"),
        P("mp", "ctx"),
        P("mp", "ctx"),
        P(None, None, None, "mp"),
        P("mp", None),
        P("mp", None),
        P("mp", None),
        P("mp"),
    )
    out_specs = P("mp", "ctx")
    return jax.shard_map(
        per_device, mesh=mesh, in_specs=in_specs, out_specs=out_specs, check_vma=False
    )
```

profile of v0, /device:TPU:0, one launch (start us, length us, event | category | flops | bytes accessed | tf_op | source)
XLA Modules:
  0.0 504.7 jit_solution(5906593025734172335)
XLA Ops:
  10.0 4.1 copy.195
  14.1 3.1 slice.630
  17.2 16.7 %reshape.270 = bf16[64,128,383]{2,1,0:T(8,128)(2,1)} reshape(bf16[64,49024]{1,0:T(8,128)(2,1)} %slice.630) | data formatting | bytes 12550144 | tf_op jit(solution)/shard_map/reshape | solution.py:37
  33.8 4.7 slice.631
  38.5 6.4 %copy.189 = bf16[64,128,256]{1,2,0:T(8,128)(2,1)} copy(bf16[64,128,256]{2,1,0:T(8,128)(2,1)} %slice.631) | data formatting | bytes 8388608
  45.3 8.1 %maximum_convert_fusion.3 = (f32[1024,2050]{1,0:T(8,128)S(1)}, f32[1024,2050]{1,0:T(8,128)}) fusion(bf16[1024,2048]{1,0:T(8,128)(2,1)} %param.11, bf16[1024,2]{1,0:T(8,128)(2,1)S(1)} %copy.174, bf16[1024,2048]{1,0:T(8,128)(2,1)} %param.12, bf16[1024,2]{1,0:T(8,128)(2,1)S(1)} %copy.175), kind=kLoop, calls=%fused_computation.43 | loop fusion | flops 16793600 | bytes 25190400 | tf_op jit(solution)/shard_map/convert_element_type | solution.py:18
  53.5 16.1 %fusion.6 = bf16[1024,2048]{1,0:T(8,128)(2,1)S(1)} fusion(f32[1024,2050]{1,0:T(8,128)} %get-tuple-element.81, f32[1024,2050]{1,0:T(8,128)S(1)} %get-tuple-element.80, f32[1024]{0:T(1024)S(1)} %bitcast.95, f32[1024]{0:T(1024)S(1)} %bitcast.96, f32[1024]{0:T(1024)S(1)} %bitcast.97, f32[1024]{0:T(1024)S(1)} %bitcast.98, f32[1024]{0:T(1024)S(1)} %bitcast.99, ...), kind=kLoop, calls=%fused_computation.10 | loop fusion | flops 25165824 | bytes 54550528 | tf_op jit(solution)/shard_map/convert_element_type | solution.py:155
  71.7 7.4 %reshape.271 = bf16[64,256,128]{2,1,0:T(8,128)(2,1)} reshape(bf16[1024,2048]{1,0:T(8,128)(2,1)} %copy-done) | data formatting | bytes 8388608 | tf_op jit(solution)/shard_map/reshape | solution.py:50
  79.1 4.5 collective-permute-start.1
  83.8 8.0 %maximum_convert_fusion.2 = f32[1024,2050]{1,0:T(8,128)} fusion(bf16[1024,2048]{1,0:T(8,128)(2,1)} %param.10, bf16[1024,2]{1,0:T(8,128)(2,1)S(1)} %copy.173), kind=kLoop, calls=%fused_computation.42 | loop fusion | flops 8396800 | bytes 12595200 | tf_op jit(solution)/shard_map/convert_element_type | solution.py:18
  91.8 4.5 fusion.19
  96.5 4.8 pad_maximum_fusion
  101.2 7.4 %reshape.269 = bf16[64,256,128]{2,1,0:T(8,128)(2,1)} reshape(bf16[1024,2048]{1,0:T(8,128)(2,1)} %pad_maximum_fusion) | data formatting | bytes 8388608 | tf_op jit(solution)/shard_map/reshape | solution.py:47
  108.6 9.7 %convolution_add_fusion = f32[64,256,128]{2,1,0:T(8,128)} fusion(f32[64,256,128]{2,1,0:T(8,128)} %fusion.19, bf16[64,256,128]{2,1,0:T(8,128)(2,1)} %reshape.269, bf16[64,256,128]{2,1,0:T(8,128)(2,1)} %bitcast.72), kind=kOutput, calls=%fused_computation.47 | convolution fusion | flops 538968064 | bytes 23068672 | tf_op jit(solution)/shard_map/gmk,gki->gmi/dot_general | solution.py:53
  118.3 9.3 %reshape.272 = f32[1024,2048]{1,0:T(8,128)} reshape(f32[64,256,128]{2,1,0:T(8,128)} %convolution_add_fusion) | data formatting | bytes 16777216 | tf_op jit(solution)/shard_map/reshape | solution.py:59
  127.7 14.1 %fusion.12 = bf16[1024,2048]{1,0:T(8,128)(2,1)S(1)} fusion(f32[1024,2048]{1,0:T(8,128)} %reshape.272, f32[1024,2050]{1,0:T(8,128)} %maximum_convert_fusion.2, f32[1024]{0:T(1024)S(1)} %bitcast.92, f32[1024]{0:T(1024)S(1)} %bitcast.93, f32[1024]{0:T(1024)S(1)} %bitcast.94), kind=kLoop, calls=%fused_computation.22 | loop fusion | flops 14680064 | bytes 37761024 | tf_op jit(solution)/shard_map/convert_element_type | solution.py:158
  144.3 4.4 maximum_convert_fusion.1
  148.7 5.4 %maximum_convert_fusion.5 = f32[1024,2050]{1,0:T(8,128)} fusion(bf16[1024,2048]{1,0:T(8,128)(2,1)S(1)} %fusion.12, bf16[1024,2]{1,0:T(8,128)(2,1)S(1)} %collective-permute-done.2), kind=kLoop, calls=%fused_computation.45 | loop fusion | flops 8396800 | bytes 12595200 | tf_op jit(solution)/shard_map/convert_element_type | solution.py:18
  154.1 17.3 %fusion.2 = bf16[1024,2048]{1,0:T(8,128)(2,1)} fusion(f32[1024,2050]{1,0:T(8,128)} %maximum_convert_fusion.5, f32[1024,2050]{1,0:T(8,128)S(1)} %maximum_convert_fusion.1, f32[1024]{0:T(1024)S(1)} %bitcast.90, f32[1024]{0:T(1024)S(1)} %bitcast.91, f32[1024]{0:T(1024)S(1)} %bitcast.86, f32[1024]{0:T(1024)S(1)} %bitcast.87, f32[1024]{0:T(1024)S(1)} %bitcast.88, ...), kind=kLoop, calls=%fused_computation.3 | loop fusion | flops 25165824 | bytes 54550528 | tf_op jit(solution)/shard_map/convert_element_type | solution.py:168
  171.5 9.4 %all-to-all-start = ((bf16[32,32,2048]{2,1,0:T(8,128)(2,1)}), bf16[32,32,2048]{2,1,0:T(8,128)(2,1)}, u32[]{:S(2)}, u32[]{:S(2)}) async-start(bf16[32,32,2048]{2,1,0:T(8,128)(2,1)} %bitcast.74), calls=%async_computation | async-start | bytes 8388608 | tf_op jit(solution)/shard_map/all_to_all | solution.py:169
  184.2 50.1 %all-to-all-done = bf16[32,32,2048]{2,1,0:T(8,128)(2,1)} async-done(((bf16[32,32,2048]{2,1,0:T(8,128)(2,1)}), bf16[32,32,2048]{2,1,0:T(8,128)(2,1)}, u32[]{:S(2)}, u32[]{:S(2)}) %all-to-all-start) | async-done | bytes 4194336 | tf_op jit(solution)/shard_map/all_to_all | solution.py:169
  234.3 6.5 %copy.177 = bf16[32,32,2048]{2,1,0:T(8,128)(2,1)} copy(bf16[32,32,2048]{2,0,1:T(8,128)(2,1)} %bitcast.30) | data formatting | bytes 8388608 | tf_op jit(solution)/shard_map/all_to_all | solution.py:169
  240.8 7.4 %reshape_reshape.4 = bf16[2,4096,256]{2,1,0:T(8,128)(2,1)} reshape(bf16[32,32,2048]{2,1,0:T(8,128)(2,1)} %copy.177) | data formatting | bytes 8388608 | tf_op jit(solution)/shard_map/reshape;reshape | solution.py:95
  248.2 3.4 fusion.78
  252.3 9.0 %slice.560 = f32[2,16,128,16]{2,3,1,0:T(8,128)S(1)} slice(f32[2,16,255,16]{2,3,1,0:T(8,128)S(1)} %copy.193), slice={[0:2:1], [0:16:1], [0:255:2], [0:16:1]} | slice | bytes 524288 | tf_op jit(solution)/shard_map/slice | solution.py:114
  261.6 9.0 %slice.559 = f32[2,16,128,16]{2,3,1,0:T(8,128)S(1)} slice(f32[2,16,256,16]{2,3,1,0:T(8,128)S(1)} %pad_maximum_fusion.1), slice={[0:2:1], [0:16:1], [0:255:2], [0:16:1]} | slice | bytes 524288 | tf_op jit(solution)/shard_map/slice | solution.py:114
  270.6 4.6 slice.564
  275.3 4.7 slice.565
  302.0 4.6 slice.605
  306.7 9.0 %slice.607 = f32[2,16,127,16]{2,3,1,0:T(8,128)S(1)} slice(f32[2,16,255,16]{2,3,1,0:T(8,128)S(1)} %copy.193), slice={[0:2:1], [0:16:1], [1:255:2], [0:16:1]} | slice | bytes 520192 | tf_op jit(solution)/shard_map/slice | solution.py:114
  335.2 3.2 pad.58
  338.5 3.3 pad.59
  342.0 4.4 pad.61
  346.6 4.3 pad.60
  351.2 6.4 %pad.62 = f32[2,16,128,16]{2,3,1,0:T(8,128)S(1)} pad(f32[2,16,64,16]{2,3,1,0:T(8,128)S(1)} %pad_maximum_fusion.7, f32[]{:T(128)} %constant.6.clone.1), padding=0_0_0x0_0_0x0_1_1x0_0_0 | pad | bytes 393220 | tf_op jit(solution)/shard_map/pad | solution.py:114
  357.7 6.5 %pad.63 = f32[2,16,128,16]{2,3,1,0:T(8,128)S(1)} pad(f32[2,16,64,16]{2,3,1,0:T(8,128)S(1)} %add.253, f32[]{:T(128)} %constant.6.clone.1), padding=0_0_0x0_0_0x1_0_1x0_0_0 | pad | bytes 393220 | tf_op jit(solution)/shard_map/pad | solution.py:114
  364.2 10.8 %pad.139 = f32[2,16,256,16]{2,3,1,0:T(8,128)S(1)} pad(f32[2,16,128,16]{2,3,1,0:T(8,128)S(1)} %add.255, f32[]{:T(128)} %constant.6.clone.1), padding=0_0_0x0_0_0x1_0_1x0_0_0 | pad | bytes 786436
  375.2 10.8 %pad.102 = f32[2,16,255,16]{2,3,1,0:T(8,128)S(1)} pad(f32[2,16,128,16]{2,3,1,0:T(8,128)S(1)} %pad_maximum_fusion.8, f32[]{:T(128)} %constant.6.clone.1), padding=0_0_0x0_0_0x0_0_1x0_0_0 | pad | bytes 784388 | tf_op jit(solution)/shard_map/slice | solution.py:115
  387.0 4.9 fusion.22
  391.9 8.6 %add_convert_fusion = bf16[2,4096,256]{2,1,0:T(8,128)(2,1)} fusion(f32[2,4096,256]{2,1,0:T(8,128)S(1)} %fusion.22, f32[2,4096,16]{1,2,0:T(8,128)S(1)} %reshape.274, f32[2,16]{1,0:T(2,128)S(1)} %get-tuple-element.66, f32[2,16]{1,0:T(2,128)S(1)} %get-tuple-element.77, f32[2,16]{1,0:T(2,128)S(1)} %get-tuple-element.72), kind=kOutput, calls=%fused_computation.39 | convolution fusion | flops 406872064 | bytes 13107584 | tf_op jit(solution)/shard_map/dkp,dps->dks/dot_general | solution.py:116
  400.5 7.4 %convert_element_type.102 = bf16[32,32,2048]{2,1,0:T(8,128)(2,1)} reshape(bf16[2,4096,256]{2,1,0:T(8,128)(2,1)} %add_convert_fusion) | data formatting | bytes 8388608 | tf_op jit(solution)/shard_map/convert_element_type | solution.py:180
  407.9 6.5 %copy.183 = bf16[32,32,2048]{2,0,1:T(8,128)(2,1)} copy(bf16[32,32,2048]{2,1,0:T(8,128)(2,1)} %convert_element_type.102) | data formatting | bytes 8388608 | tf_op jit(solution)/shard_map/convert_element_type | solution.py:180
  414.4 4.9 all-to-all-start.1
  419.5 7.8 %maximum_convert_fusion = f32[1024,2050]{1,0:T(8,128)} fusion(bf16[1024,2048]{1,0:T(8,128)(2,1)} %param.13, bf16[1024,2]{1,0:T(8,128)(2,1)S(1)} %copy.171), kind=kLoop, calls=%fused_computation.40 | loop fusion | flops 8396800 | bytes 12595200 | tf_op jit(solution)/shard_map/convert_element_type | solution.py:18
  427.3 45.5 %all-to-all-done.1 = bf16[32,32,2048]{2,0,1:T(8,128)(2,1)} async-done(((bf16[32,32,2048]{2,0,1:T(8,128)(2,1)}), bf16[32,32,2048]{2,0,1:T(8,128)(2,1)}, u32[]{:S(2)}, u32[]{:S(2)}) %all-to-all-start.1) | async-done | bytes 4194336 | tf_op jit(solution)/shard_map/all_to_all | solution.py:181
  472.8 14.5 %multiply_reduce_fusion = (f32[2048]{0:T(1024)S(1)}, f32[1024,2048]{1,0:T(8,128)}) fusion(bf16[32,32,2048]{2,0,1:T(8,128)(2,1)} %all-to-all-done.1, f32[1024,2050]{1,0:T(8,128)} %maximum_convert_fusion, f32[1024]{0:T(1024)S(1)} %bitcast.84, f32[1024]{0:T(1024)S(1)} %bitcast.85, f32[1024]{0:T(1024)S(1)} %bitcast.83), kind=kLoop, calls=%fused_computation.38 | loop fusion | flops 18872320 | bytes 37769216 | tf_op jit(solution)/shard_map/reduce_sum | solution.py:183
  487.2 10.8 %psum.7 = f32[2048]{0:T(1024)S(1)} all-reduce(f32[2048]{0:T(1024)S(1)} %get-tuple-element.37), channel_id=1, replica_groups=mesh['ctx'=32,'mp'=4] {'mp'}, use_global_device_ids=true, to_apply=%region_1.2 | all-reduce | flops 2048 | bytes 16384 | tf_op jit(solution)/shard_map/psum | solution.py:184
  498.1 6.2 %multiply_convert_fusion = bf16[1024,2048]{1,0:T(8,128)(2,1)} fusion(f32[1024,2048]{1,0:T(8,128)} %get-tuple-element.38, f32[1024]{0:T(1024)S(1)} %copy-done.6, f32[2048]{0:T(1024)S(1)} %add_rsqrt_fusion), kind=kLoop, calls=%fused_computation.37 | loop fusion | flops 6291456 | bytes 12595200 | tf_op jit(solution)/shard_map/convert_element_type | solution.py:186
  (169 shorter events, 63.1 us)
Async XLA Ops:
  6.2 38.7 %collective-permute-start = (bf16[5,1024,2]{1,2,0:T(2,128)(2,1)S(1)}, bf16[5,1024,2]{1,2,0:T(2,128)(2,1)S(1)}, u32[]{:S(2)}, u32[]{:S(2)}) collective-permute-start(bf16[5,1024,2]{1,2,0:T(2,128)(2,1)S(1)} %constant_dynamic-update-slice_fusion), channel_id=1, source_target_pairs={{0,4},{4,8},{8,12},{12,16},{16,20},{20,24},{24,28},{28,32},{32,36}... | collective-permute-start | bytes 61448 | tf_op jit(solution)/shard_map/ppermute | solution.py:14
  69.6 2.0 copy-start
  79.1 17.3 %collective-permute-start.1 = (bf16[1024,128]{1,0:T(8,128)(2,1)S(1)}, bf16[1024,128]{1,0:T(8,128)(2,1)S(1)}, u32[]{:S(2)}, u32[]{:S(2)}) collective-permute-start(bf16[1024,128]{1,0:T(8,128)(2,1)S(1)} %slice.629), channel_id=1, source_target_pairs={{0,4},{4,8},{8,12},{12,16},{16,20},{20,24},{24,28},{28,32},{32,36}... | collective-permute-start | bytes 786440 | tf_op jit(solution)/shard_map/ppermute | solution.py:14
  83.8 8.0 %copy-start.1 = (bf16[64,256,128]{2,1,0:T(8,128)(2,1)S(1)}, bf16[64,256,128]{2,1,0:T(8,128)(2,1)}, u32[]{:S(2)}) copy-start(bf16[64,256,128]{2,1,0:T(8,128)(2,1)} %reshape.271) | copy-start | bytes 12582916
  83.8 8.0 %copy-start.2 = (bf16[64,128,256]{1,2,0:T(8,128)(2,1)S(1)}, bf16[64,128,256]{1,2,0:T(8,128)(2,1)}, u32[]{:S(2)}) copy-start(bf16[64,128,256]{1,2,0:T(8,128)(2,1)} %copy.189) | copy-start | bytes 12582916
  141.9 6.8 %collective-permute-start.2 = (bf16[1024,2]{1,0:T(8,128)(2,1)S(1)}, bf16[1024,2]{1,0:T(8,128)(2,1)S(1)}, u32[]{:S(2)}, u32[]{:S(2)}) collective-permute-start(bf16[1024,2]{1,0:T(8,128)(2,1)S(1)} %slice.634), channel_id=1, source_target_pairs={{0,4},{4,8},{8,12},{12,16},{16,20},{20,24},{24,28},{28,32},{32,36}... | collective-permute-start | bytes 12296 | tf_op jit(solution)/shard_map/ppermute | solution.py:14
  171.5 9.4 %copy-start.4 = (f32[64,16]{0,1:T(8,128)S(1)}, f32[64,16]{0,1:T(8,128)}, u32[]{:S(2)}) copy-start(f32[64,16]{0,1:T(8,128)} %param.17) | copy-start | bytes 12292
  171.5 9.4 %copy-start.5 = (f32[64,16]{0,1:T(8,128)S(1)}, f32[64,16]{0,1:T(8,128)}, u32[]{:S(2)}) copy-start(f32[64,16]{0,1:T(8,128)} %param.18) | copy-start | bytes 12292
  171.5 62.8 %all-to-all-start = ((bf16[32,32,2048]{2,1,0:T(8,128)(2,1)}), bf16[32,32,2048]{2,1,0:T(8,128)(2,1)}, u32[]{:S(2)}, u32[]{:S(2)}) async-start(bf16[32,32,2048]{2,1,0:T(8,128)(2,1)} %bitcast.74), calls=%async_computation | async-start | bytes 8388608 | tf_op jit(solution)/shard_map/all_to_all | solution.py:169
  338.5 48.3 %copy-start.3 = (f32[256,256]{1,0:T(8,128)S(1)}, f32[256,256]{1,0:T(8,128)}, u32[]{:S(2)}) copy-start(f32[256,256]{1,0:T(8,128)} %clamp_convert_fusion) | copy-start | bytes 786436
  338.5 48.3 %copy-start.7 = (f32[2]{0:T(128)S(1)}, f32[2]{0:T(128)}, u32[]{:S(2)}) copy-start(f32[2]{0:T(128)} %get-tuple-element.12) | copy-start | bytes 28
  338.5 48.3 %copy-start.8 = (f32[2]{0:T(128)S(1)}, f32[2]{0:T(128)}, u32[]{:S(2)}) copy-start(f32[2]{0:T(128)} %get-tuple-element.13) | copy-start | bytes 28
  338.5 48.3 %copy-start.9 = (f32[2]{0:T(128)S(1)}, f32[2]{0:T(128)}, u32[]{:S(2)}) copy-start(f32[2]{0:T(128)} %get-tuple-element.14) | copy-start | bytes 28
  341.8 45.0 %copy-start.10 = (f32[2]{0:T(128)S(1)}, f32[2]{0:T(128)}, u32[]{:S(2)}) copy-start(f32[2]{0:T(128)} %get-tuple-element.15) | copy-start | bytes 28
  341.8 45.0 %copy-start.11 = (f32[2]{0:T(128)S(1)}, f32[2]{0:T(128)}, u32[]{:S(2)}) copy-start(f32[2]{0:T(128)} %get-tuple-element.16) | copy-start | bytes 28
  341.8 45.0 %copy-start.12 = (f32[2]{0:T(128)S(1)}, f32[2]{0:T(128)}, u32[]{:S(2)}) copy-start(f32[2]{0:T(128)} %get-tuple-element.17) | copy-start | bytes 28
  341.8 45.0 %copy-start.13 = (f32[2]{0:T(128)S(1)}, f32[2]{0:T(128)}, u32[]{:S(2)}) copy-start(f32[2]{0:T(128)} %get-tuple-element.18) | copy-start | bytes 28
  341.8 45.0 %copy-start.14 = (f32[2]{0:T(128)S(1)}, f32[2]{0:T(128)}, u32[]{:S(2)}) copy-start(f32[2]{0:T(128)} %get-tuple-element.19) | copy-start | bytes 28
  341.8 45.0 %copy-start.15 = (f32[2]{0:T(128)S(1)}, f32[2]{0:T(128)}, u32[]{:S(2)}) copy-start(f32[2]{0:T(128)} %get-tuple-element.20) | copy-start | bytes 28
  341.8 45.0 %copy-start.16 = (f32[2]{0:T(128)S(1)}, f32[2]{0:T(128)}, u32[]{:S(2)}) copy-start(f32[2]{0:T(128)} %get-tuple-element.21) | copy-start | bytes 28
  341.8 45.0 %copy-start.17 = (f32[2]{0:T(128)S(1)}, f32[2]{0:T(128)}, u32[]{:S(2)}) copy-start(f32[2]{0:T(128)} %get-tuple-element.22) | copy-start | bytes 28
  341.9 45.0 %copy-start.18 = (f32[2]{0:T(128)S(1)}, f32[2]{0:T(128)}, u32[]{:S(2)}) copy-start(f32[2]{0:T(128)} %get-tuple-element.23) | copy-start | bytes 28
  341.9 45.0 %copy-start.19 = (f32[2]{0:T(128)S(1)}, f32[2]{0:T(128)}, u32[]{:S(2)}) copy-start(f32[2]{0:T(128)} %get-tuple-element.24) | copy-start | bytes 28
  341.9 45.0 %copy-start.20 = (f32[2]{0:T(128)S(1)}, f32[2]{0:T(128)}, u32[]{:S(2)}) copy-start(f32[2]{0:T(128)} %get-tuple-element.25) | copy-start | bytes 28
  341.9 45.0 %copy-start.21 = (f32[2]{0:T(128)S(1)}, f32[2]{0:T(128)}, u32[]{:S(2)}) copy-start(f32[2]{0:T(128)} %get-tuple-element.26) | copy-start | bytes 28
  341.9 45.0 %copy-start.22 = (f32[2]{0:T(128)S(1)}, f32[2]{0:T(128)}, u32[]{:S(2)}) copy-start(f32[2]{0:T(128)} %get-tuple-element.27) | copy-start | bytes 28
  341.9 45.0 %copy-start.23 = (f32[2]{0:T(128)S(1)}, f32[2]{0:T(128)}, u32[]{:S(2)}) copy-start(f32[2]{0:T(128)} %get-tuple-element.28) | copy-start | bytes 28
  341.9 45.0 %copy-start.24 = (f32[2]{0:T(128)S(1)}, f32[2]{0:T(128)}, u32[]{:S(2)}) copy-start(f32[2]{0:T(128)} %get-tuple-element.29) | copy-start | bytes 28
  341.9 45.0 %copy-start.25 = (f32[2]{0:T(128)S(1)}, f32[2]{0:T(128)}, u32[]{:S(2)}) copy-start(f32[2]{0:T(128)} %get-tuple-element.30) | copy-start | bytes 28
  341.9 45.0 %copy-start.26 = (f32[2]{0:T(128)S(1)}, f32[2]{0:T(128)}, u32[]{:S(2)}) copy-start(f32[2]{0:T(128)} %get-tuple-element.31) | copy-start | bytes 28
  341.9 45.0 %copy-start.27 = (f32[2]{0:T(128)S(1)}, f32[2]{0:T(128)}, u32[]{:S(2)}) copy-start(f32[2]{0:T(128)} %get-tuple-element.32) | copy-start | bytes 28
  342.0 45.0 %copy-start.28 = (f32[2]{0:T(128)S(1)}, f32[2]{0:T(128)}, u32[]{:S(2)}) copy-start(f32[2]{0:T(128)} %get-tuple-element.33) | copy-start | bytes 28
  342.0 45.0 %copy-start.29 = (f32[2]{0:T(128)S(1)}, f32[2]{0:T(128)}, u32[]{:S(2)}) copy-start(f32[2]{0:T(128)} %get-tuple-element.34) | copy-start | bytes 28
  342.0 45.0 %copy-start.30 = (f32[2]{0:T(128)S(1)}, f32[2]{0:T(128)}, u32[]{:S(2)}) copy-start(f32[2]{0:T(128)} %get-tuple-element.35) | copy-start | bytes 28
  342.0 45.0 %copy-start.31 = (f32[2]{0:T(128)S(1)}, f32[2]{0:T(128)}, u32[]{:S(2)}) copy-start(f32[2]{0:T(128)} %get-tuple-element.36) | copy-start | bytes 28
  414.4 58.3 %all-to-all-start.1 = ((bf16[32,32,2048]{2,0,1:T(8,128)(2,1)}), bf16[32,32,2048]{2,0,1:T(8,128)(2,1)}, u32[]{:S(2)}, u32[]{:S(2)}) async-start(bf16[32,32,2048]{2,0,1:T(8,128)(2,1)} %copy.183), calls=%async_computation.1 | async-start | bytes 8388608 | tf_op jit(solution)/shard_map/all_to_all | solution.py:181
  472.8 25.3 %copy-start.6 = (f32[1024]{0:T(1024)S(1)}, f32[1024]{0:T(1024)}, u32[]{:S(2)}) copy-start(f32[1024]{0:T(1024)} %param.19) | copy-start | bytes 12292
where the time goes:
time: 512 us; the launch traced here: 505 us
  local copies, waits for them, and re-layouts  227 us (44%)
  other arithmetic  117 us (23%)
  waiting for transfers between devices  95.6 us (19%)
  matrix products  31.1 us (6%)
  starting transfers between devices  22.4 us (4%)
  blocking collectives  10.8 us (2%)
    slice x20, local copies, waits for them, and re-layouts, long_filter(): lax.associative_scan(chain_pair, (factor, local_partial_terms), axis=2)  61 us
    all_to_all x1, waiting for transfers between devices, per_device(): lax.all_to_all(second, 'ctx', split_axis=0, concat_axis=1, tiled=True)  50.1 us
    all_to_all x1, waiting for transfers between devices, per_device(): lax.all_to_all(share_result, 'ctx', split_axis=1, concat_axis=0, tiled=True)  45.5 us
    pad x12, local copies, waits for them, and re-layouts, long_filter(): lax.associative_scan(chain_pair, (factor, local_partial_terms), axis=2)  42.6 us
    convert_element_type x5, other arithmetic, short_filter(): as_float = extended.astype(jnp.float32)  33.7 us
    unnamed x81, local copies, waits for them, and re-layouts  25 us
    convert_element_type x1, other arithmetic, per_device(): second = (key_next * value_next).astype(jnp.bfloat16)  17.3 us
    reshape x1, local copies, waits for them, and re-layouts, medium_kernel(): tiled.reshape(group_count, tap_count, 3 * tap_count - 1)  16.7 us
  transfers between devices with their start and end apart: 5, of which 2 were waited for; matrix products, arithmetic and copies ran while one was open for 13% of the time, Pallas kernels for 0%

commit v1 on v0

v1 whole, which is shorter than its diff:
```python
import functools

import jax
import jax.numpy as jnp
from jax import lax
from jax.experimental import pallas as pl
from jax.experimental.pallas import tpu as pltpu
from jax.sharding import PartitionSpec as P

GROUP = 16
TAPS = 128
BLOCK = 256
MODES = 16
LANES = 128
MESH = pl.DeviceIdType.MESH
F32 = jnp.float32
BF16 = jnp.bfloat16
Q1, K1, V1, K2, Q2 = range(5)


def aligned(index, size):
    return pl.ds(pl.multiple_of(index * size, size), size)


def lane_ids(rows, cols):
    return lax.broadcasted_iota(jnp.int32, (rows, cols), 1)


def split_pair(x):
    high = x.astype(BF16)
    low = (x - high.astype(F32)).astype(BF16)
    return high, low


def short_filter(x, taps):
    w0, w1, w2 = taps
    return w0 * x + w1 * pltpu.roll(x, 1, 1) + w2 * pltpu.roll(x, 2, 1)


def to_rows(x, first, count, step, width):
    return jnp.concatenate(
        [x[:, first + i * step : first + i * step + width] for i in range(count)], axis=0
    )


def kernel(
    n_ctx, n_mp, q1, k1, v1, k2, q2, cw, mr, rate, residue, gain, out,
    xin, hwide, hthin, wmed, wlong, readout, proj, ptwo, within, qnext, state, wcol,
    pad, tapf, rate_t, res_t, fin, decay, got, carry, back, sums, sums_in,
    in_sem, hsend, hrecv, asend, arecv, bsend, brecv, msend, mrecv, osem,
):
    me = lax.axis_index("ctx")
    my_mp = lax.axis_index("mp")
    right = lax.rem(me + 1, n_ctx)
    chans, length = xin.shape[1:]
    tiles = chans // LANES
    per_tile = LANES // GROUP
    groups = chans // GROUP
    blocks = length // BLOCK
    med_blocks = length // TAPS
    share = tiles * MODES // n_ctx
    cuts = MODES // share
    streams = (q1, k1, v1, k2, q2)

    def load_copy(s, t):
        rows = aligned(t, LANES)
        return pltpu.make_async_copy(streams[s].at[rows, :], xin.at[s, rows, :], in_sem.at[s, t])

    def halo_copy(s, t):
        rows = aligned(t, LANES)
        wide = s in (K1, V1)
        width = 2 * LANES if wide else LANES
        target = hwide.at[s - K1, rows, :] if wide else hthin.at[{Q1: 0, K2: 1, Q2: 2}[s], rows, :]
        return pltpu.make_async_remote_copy(
            src_ref=streams[s].at[rows, pl.ds(length - width, width)],
            dst_ref=target,
            send_sem=hsend.at[s, t],
            recv_sem=hrecv.at[s, t],
            device_id={"ctx": right},
            device_id_type=MESH,
        )

    first_four = (K1, V1, Q1, K2)

    def start_loads(t, _):
        for s in first_four:
            load_copy(s, t).start()
        return _

    lax.fori_loop(0, tiles, start_loads, 0)

    def start_late(t, _):
        load_copy(Q2, t).start()
        return _

    lax.fori_loop(0, tiles, start_late, 0)

    barrier = pltpu.get_barrier_semaphore()

    def greet_ctx(i, _):
        pl.semaphore_signal(
            barrier, inc=1, device_id={"ctx": lax.rem(me + i, n_ctx)}, device_id_type=MESH
        )
        return _

    lax.fori_loop(1, n_ctx, greet_ctx, 0)
    for i in range(1, n_mp):
        pl.semaphore_signal(
            barrier, inc=1, device_id={"mp": lax.rem(my_mp + i, n_mp)}, device_id_type=MESH
        )

    pad[...] = jnp.zeros_like(pad)
    for layer in range(2):
        for stream in range(3):
            for tap in range(3):
                at = layer * 9 + stream * 3 + tap
                pad[at : at + 1, :] = cw[layer, stream, tap : tap + 1, :]
    pad[18:19, :] = gain[...]
    for t in range(tiles):
        wcol[t * LANES : (t + 1) * LANES, :] = pad[:, t * LANES : (t + 1) * LANES].T
    tapf[...] = mr[...].astype(F32)
    pad[...] = jnp.zeros_like(pad)
    pad[0:groups, 0:MODES] = rate[...]
    rate_t[...] = pad[:, 0:LANES].T[0:MODES, :]
    pad[0:groups, 0:MODES] = residue[...]
    res_t[...] = pad[:, 0:LANES].T[0:MODES, :]

    def mode_column(table, g):
        hit = lane_ids(MODES, LANES) == g
        return jnp.sum(jnp.where(hit, table[...], 0.0), axis=1, keepdims=True)

    def circulant(row):
        return pltpu.roll(
            jnp.broadcast_to(row, (LANES, LANES)), 0, 1, stride=1, stride_axis=0
        )

    def tables(g, _):
        above = lane_ids(LANES, LANES) >= lax.broadcasted_iota(jnp.int32, (LANES, LANES), 0)
        rate_c = mode_column(rate_t, g)
        amp = mode_column(res_t, g) * jnp.sqrt(rate_c)
        lag = lane_ids(1, BLOCK).astype(F32)
        fall = jnp.exp(-rate_c * lag)
        proj[g] = jnp.exp(-rate_c * (float(BLOCK - 1) - lag)).astype(BF16)
        tall = amp * fall
        high, low = split_pair(tall * jnp.exp(-rate_c))
        readout[g] = jnp.concatenate([high, low, high], axis=0)
        taps_h = jnp.sum(tall, axis=0, keepdims=True)
        near = circulant(taps_h[:, :LANES])
        far = circulant(taps_h[:, LANES:])
        diagonal = jnp.where(above, near, 0.0).astype(BF16)
        wlong[g, 0:LANES, 0:LANES] = diagonal
        wlong[g, LANES:, LANES:] = diagonal
        wlong[g, 0:LANES, LANES:] = jnp.where(above, far, near).astype(BF16)
        wlong[g, LANES:, 0:LANES] = jnp.zeros((LANES, LANES), BF16)
        short = circulant(tapf[pl.ds(g, 1), :])
        wmed[g, 0:LANES, :] = jnp.where(above, 0.0, short).astype(BF16)
        wmed[g, LANES:, :] = jnp.where(above, short, 0.0).astype(BF16)
        return _

    early = groups // 2
    lax.fori_loop(0, early, tables, 0)
    pl.semaphore_wait(barrier, n_ctx - 1 + n_mp - 1)

    def start_halos(t, _):
        for s in first_four:
            halo_copy(s, t).start()
        return _

    lax.fori_loop(0, tiles, start_halos, 0)

    def start_late_halos(t, _):
        halo_copy(Q2, t).start()
        return _

    lax.fori_loop(0, tiles, start_late_halos, 0)
    lax.fori_loop(early, groups, tables, 0)

    keep = me > 0

    def columns(rows, layer, stream):
        at = layer * 9 + stream * 3
        return [wcol[rows, at + tap : at + tap + 1] for tap in range(3)]

    def extended(s, rows):
        wide = s in (K1, V1)
        halo = hwide[s - K1, rows, :] if wide else hthin[{Q1: 0, K2: 1, Q2: 2}[s], rows, :]
        halo = jnp.where(keep, halo.astype(F32), 0.0)
        return jnp.concatenate([halo, xin[s, rows, :].astype(F32)], axis=1)

    def produce(g, t, i):
        rows = aligned(g, GROUP)
        key = short_filter(extended(K1, rows), columns(rows, 0, 1))
        value = short_filter(extended(V1, rows), columns(rows, 0, 2))
        product = (key * value).astype(BF16)
        mixed = jnp.dot(
            to_rows(product, 0, med_blocks + 1, TAPS, 2 * TAPS), wmed[g], preferred_element_type=F32
        )
        mixed = jnp.concatenate(
            [mixed[j * GROUP : (j + 1) * GROUP, :] for j in range(med_blocks + 1)], axis=1
        )
        query = short_filter(extended(Q1, rows), columns(rows, 0, 0))
        layer_one = (query * mixed).astype(BF16).astype(F32)
        value_two = short_filter(layer_one, columns(rows, 1, 2))[:, LANES:]
        key_two = short_filter(extended(K2, rows), columns(rows, 1, 1))[:, LANES:]
        second = (key_two * value_two).astype(BF16)
        pieces = to_rows(second, 0, blocks, BLOCK, BLOCK)
        ptwo[g] = pieces
        local = lax.dot_general(
            proj[g], pieces, (((1,), (1,)), ((), ())), preferred_element_type=F32
        )
        rate_c = mode_column(rate_t, g)
        lane = lane_ids(MODES, GROUP * blocks)
        total = local
        width = 1
        while width < blocks:
            moved = pltpu.roll(total, width * GROUP, 1)
            factor = jnp.exp(-rate_c * float(BLOCK * width))
            total = total + jnp.where(lane >= width * GROUP, factor * moved, 0.0)
            width *= 2
        state[g] = jnp.where(lane >= GROUP, pltpu.roll(total, GROUP, 1), 0.0)
        spot = lax.shift_right_logical(lane, 4) == i
        moved = pltpu.roll(total, lax.rem(i * GROUP + GROUP, LANES), 1)
        drop = jnp.exp(-rate_c * float(length))
        for c in range(cuts):
            part = slice(c * share, (c + 1) * share)
            at = t * cuts + c
            fin[at] = jnp.where(spot[part], moved[part], fin[at])
            decay[at] = jnp.where(spot[part], jnp.broadcast_to(drop, moved.shape)[part], decay[at])

    fin[...] = jnp.zeros_like(fin)
    decay[...] = jnp.zeros_like(decay)

    def tile_step(t, _):
        for s in first_four:
            load_copy(s, t).wait()
            halo_copy(s, t).wait_recv()

        def group_step(i, _):
            produce(t * per_tile + i, t, i)
            return _

        return lax.fori_loop(0, per_tile, group_step, _)

    lax.fori_loop(0, tiles, tile_step, 0)

    def state_copy(peer):
        return pltpu.make_async_remote_copy(
            src_ref=fin.at[peer],
            dst_ref=got.at[me],
            send_sem=asend.at[peer],
            recv_sem=arecv.at[me],
            device_id={"ctx": peer},
            device_id_type=MESH,
        )

    def state_arrival(peer):
        return pltpu.make_async_remote_copy(
            src_ref=fin.at[peer],
            dst_ref=got.at[peer],
            send_sem=asend.at[peer],
            recv_sem=arecv.at[peer],
            device_id={"ctx": peer},
            device_id_type=MESH,
        )

    def carry_copy(peer):
        return pltpu.make_async_remote_copy(
            src_ref=carry.at[peer],
            dst_ref=back.at[me],
            send_sem=bsend.at[peer],
            recv_sem=brecv.at[me],
            device_id={"ctx": peer},
            device_id_type=MESH,
        )

    def carry_arrival(peer):
        return pltpu.make_async_remote_copy(
            src_ref=carry.at[peer],
            dst_ref=back.at[peer],
            send_sem=bsend.at[peer],
            recv_sem=brecv.at[peer],
            device_id={"ctx": peer},
            device_id_type=MESH,
        )

    def each_peer(act):
        def step(i, _):
            act(lax.rem(me + i, n_ctx))
            return _

        lax.fori_loop(1, n_ctx, step, 0)

    each_peer(lambda peer: state_copy(peer).start())
    got[me] = fin[me]

    def inner_part(t, _):
        load_copy(Q2, t).wait()
        halo_copy(Q2, t).wait_recv()

        def group_step(i, _):
            g = t * per_tile + i
            rows = aligned(g, GROUP)
            within[g] = jnp.dot(ptwo[g], wlong[g], preferred_element_type=F32)
            query = short_filter(extended(Q2, rows), columns(rows, 1, 0))[:, LANES:]
            qnext[g] = to_rows(query, 0, blocks, BLOCK, BLOCK)
            return _

        return lax.fori_loop(0, per_tile, group_step, _)

    half = (tiles + 1) // 2
    lax.fori_loop(0, half, inner_part, 0)
    each_peer(lambda peer: state_arrival(peer).wait_recv())

    def chain(d, value):
        carry[d] = value
        return value * decay[me] + got[d]

    lax.fori_loop(0, n_ctx, chain, jnp.zeros((share, LANES), F32))
    each_peer(lambda peer: carry_copy(peer).start())
    back[me] = carry[me]
    lax.fori_loop(half, tiles, inner_part, 0)
    each_peer(lambda peer: carry_arrival(peer).wait_recv())

    sums[...] = jnp.zeros_like(sums)

    def finish_tile(t, _):
        incoming = jnp.concatenate([back[t * cuts + c] for c in range(cuts)], axis=0)

        def group_step(i, _):
            g = t * per_tile + i
            lane = lane_ids(MODES, LANES)
            seed = jnp.where(
                lane < GROUP, pltpu.roll(incoming, lax.rem(LANES - i * GROUP, LANES), 1), 0.0
            )
            width = 1
            while width < blocks:
                seed = seed + pltpu.roll(seed, width * GROUP, 1)
                width *= 2
            rate_c = mode_column(rate_t, g)
            block_at = lax.shift_right_logical(lane, 4).astype(F32)
            total = state[g] + seed * jnp.exp(-rate_c * (block_at * float(BLOCK)))
            high, low = split_pair(total)
            stacked = jnp.concatenate([high, high, low], axis=0)
            carried = lax.dot_general(
                stacked, readout[g], (((0,), (0,)), ((), ())), preferred_element_type=F32
            )
            long_two = (within[g] + carried).astype(BF16).astype(F32)
            gated = qnext[g] * long_two
            within[g] = gated
            square = gated * gated
            for b in range(blocks):
                low_rows = square[b * GROUP : b * GROUP + 8, :]
                sums[b] = sums[b] + (low_rows + square[b * GROUP + 8 : (b + 1) * GROUP, :])
            return _

        return lax.fori_loop(0, per_tile, group_step, _)

    lax.fori_loop(0, tiles, finish_tile, 0)

    sums_in[my_mp] = jnp.sum(sums[...], axis=1)

    def sum_copy(peer, place):
        return pltpu.make_async_remote_copy(
            src_ref=sums_in.at[my_mp],
            dst_ref=sums_in.at[place],
            send_sem=msend.at[peer],
            recv_sem=mrecv.at[place],
            device_id={"mp": peer},
            device_id_type=MESH,
        )

    mp_peers = [lax.rem(my_mp + i, n_mp) for i in range(1, n_mp)]
    for peer in mp_peers:
        sum_copy(peer, my_mp).start()
    for peer in mp_peers:
        sum_copy(peer, peer).wait_recv()
    whole = sums_in[0]
    for i in range(1, n_mp):
        whole = whole + sums_in[i]
    scale = lax.rsqrt(whole / float(n_mp * chans) + 1e-05)
    sums[...] = jnp.broadcast_to(scale[:, None, :], sums.shape)

    def out_copy(t):
        rows = aligned(t, LANES)
        return pltpu.make_async_copy(xin.at[Q1, rows, :], out.at[rows, :], osem.at[t])

    def scale_tile(t, _):
        def group_step(i, _):
            g = t * per_tile + i
            rows = aligned(g, GROUP)
            gain_c = wcol[rows, 18:19]
            gated = within[g]
            for b in range(blocks):
                scale_b = jnp.concatenate([sums[b], sums[b]], axis=0)
                piece = gated[b * GROUP : (b + 1) * GROUP, :] * scale_b * gain_c
                xin[Q1, rows, b * BLOCK : (b + 1) * BLOCK] = piece.astype(BF16)
            return _

        lax.fori_loop(0, per_tile, group_step, 0)
        out_copy(t).start()
        return _

    lax.fori_loop(0, tiles, scale_tile, 0)

    for peer in mp_peers:
        sum_copy(peer, my_mp).wait_send()
    each_peer(lambda peer: state_copy(peer).wait_send())
    each_peer(lambda peer: carry_copy(peer).wait_send())

    def drain(t, _):
        for s in range(5):
            halo_copy(s, t).wait_send()
        out_copy(t).wait()
        return _

    lax.fori_loop(0, tiles, drain, 0)


def per_device(n_ctx, n_mp, query_one, key_one, value_one, query_two, key_two, conv_weights,
               mr_filter, li_rate, li_residue, norm_gain):
    chans, length = query_one.shape
    groups = chans // GROUP
    tiles = chans // LANES
    blocks = length // BLOCK
    share = tiles * MODES // n_ctx
    any_spec = pl.BlockSpec(memory_space=pl.ANY)
    vmem_spec = pl.BlockSpec(memory_space=pltpu.VMEM)
    dma = pltpu.SemaphoreType.DMA
    message = pltpu.VMEM((n_ctx, share, LANES), F32)
    return pl.pallas_call(
        functools.partial(kernel, n_ctx, n_mp),
        out_shape=jax.ShapeDtypeStruct((chans, length), BF16),
        in_specs=[any_spec] * 5 + [vmem_spec] * 5,
        out_specs=any_spec,
        scratch_shapes=[
            pltpu.VMEM((5, chans, length), BF16),
            pltpu.VMEM((2, chans, 2 * LANES), BF16),
            pltpu.VMEM((3, chans, LANES), BF16),
            pltpu.VMEM((groups, 2 * TAPS, TAPS), BF16),
            pltpu.VMEM((groups, BLOCK, BLOCK), BF16),
            pltpu.VMEM((groups, 3 * MODES, BLOCK), BF16),
            pltpu.VMEM((groups, MODES, BLOCK), BF16),
            pltpu.VMEM((groups, GROUP * blocks, BLOCK), BF16),
            pltpu.VMEM((groups, GROUP * blocks, BLOCK), F32),
            pltpu.VMEM((groups, GROUP * blocks, BLOCK), F32),
            pltpu.VMEM((groups, MODES, LANES), F32),
            pltpu.VMEM((chans, LANES), F32),
            pltpu.VMEM((LANES, chans), F32),
            pltpu.VMEM((groups, TAPS), F32),
            pltpu.VMEM((MODES, LANES), F32),
            pltpu.VMEM((MODES, LANES), F32),
            message,
            message,
            message,
            message,
            message,
            pltpu.VMEM((blocks, 8, BLOCK), F32),
            pltpu.VMEM((n_mp, blocks, BLOCK), F32),
            dma((5, tiles)),
            dma((5, tiles)),
            dma((5, tiles)),
            dma((n_ctx,)),
            dma((n_ctx,)),
            dma((n_ctx,)),
            dma((n_ctx,)),
            dma((n_mp,)),
            dma((n_mp,)),
            dma((tiles,)),
        ],
        compiler_params=pltpu.CompilerParams(
            collective_id=0, has_side_effects=True, vmem_limit_bytes=67043328
        ),
        name="hyena_pair",
    )(
        query_one, key_one, value_one, key_two, query_two,
        conv_weights, mr_filter, li_rate, li_residue, norm_gain.reshape(1, chans),
    )


def solution(mesh):
    in_specs = (
        P("mp", "ctx"),
        P("mp", "ctx"),
        P("mp", "ctx"),
        P("mp", "ctx"),
        P("mp", "ctx"),
        P(None, None, None, "mp"),
        P("mp", None),
        P("mp", None),
        P("mp", None),
        P("mp"),
    )
    return jax.shard_map(
        functools.partial(per_device, mesh.shape["ctx"], mesh.shape["mp"]),
        mesh=mesh,
        in_specs=in_specs,
        out_specs=P("mp", "ctx"),
        check_vma=False,
    )
```

time: 512 us -> 138 us (0.27); the launches traced: 505 us -> 138 us
  local copies, waits for them, and re-layouts: 227 us -> 9.12 us
  Pallas kernels: 0 us -> 129 us
  other arithmetic: 117 us -> 0 us
  waiting for transfers between devices: 95.6 us -> 0 us
  matrix products: 31.1 us -> 0 us
  starting transfers between devices: 22.4 us -> 0 us
  blocking collectives: 10.8 us -> 0 us
    pallas_call x0 -> x1, Pallas kernels: none -> 129 us  [per_device(): pl.pallas_call(functools.partial(kernel, n_ctx, n_mp), out_shape=jax.Shap...]
    all_to_all x2 -> x0, waiting for transfers between devices: 95.6 us -> none  [the longest x1 50.1 us: per_device(): lax.all_to_all(second, 'ctx', split_axis=0, concat_axis=1, tiled=True)]
    convert_element_type x10 -> x0, other arithmetic: 88.1 us -> none  [the longest x5 33.7 us: short_filter(): as_float = extended.astype(jnp.float32)]
    slice x34 -> x0, local copies, waits for them, and re-layouts: 87.4 us -> none  [the longest x20 61 us: long_filter(): lax.associative_scan(chain_pair, (factor, local_partial_terms), axis=2)]
    pad x12 -> x0, local copies, waits for them, and re-layouts: 42.6 us -> none  [long_filter(): lax.associative_scan(chain_pair, (factor, local_partial_terms), axis=2)]
    reshape x5 -> x0, local copies, waits for them, and re-layouts: 40.9 us -> none  [the longest x1 16.7 us: medium_kernel(): tiled.reshape(group_count, tap_count, 3 * tap_count - 1)]
    dot_general x5 -> x0, matrix products: 31.1 us -> none  [the longest x1 9.74 us: medium_filter(): jnp.einsum('gmk,gki->gmi', first_half, kernel[:, :tap_count], preferred_e...]
    unnamed x81 -> x4, local copies, waits for them, and re-layouts: 25 us -> 9.12 us
  transfers between devices with their start and end apart: 5 -> 0, of which waited for: 2 -> 0; matrix products, arithmetic and copies ran while one was open for 13% -> 0% of each run, Pallas kernels for 0% -> 0%
where the time goes in v1:
time: 138 us
  Pallas kernels  129 us (93%)
  local copies, waits for them, and re-layouts  9.12 us (7%)
    pallas_call x1, Pallas kernels, per_device(): pl.pallas_call(functools.partial(kernel, n_ctx, n_mp), out_shape=jax.Shap...  129 us
    unnamed x4, local copies, waits for them, and re-layouts  9.12 us

profile of v1, /device:TPU:0, one launch (start us, length us, event | category | flops | bytes accessed | tf_op | source)
XLA Modules:
  0.0 138.0 jit_solution(5605604273744774084)
XLA Ops:
  0.0 1.4 copy.12.rate
  1.4 1.4 %copy.13.residue = f32[64,16]{1,0:T(8,128)} copy(f32[64,16]{0,1:T(8,128)} %param.18) | data formatting | bytes 8192 | tf_op args[8]
  2.8 1.6 %copy.11.cw = f32[2,3,3,1024]{3,2,1,0:T(4,128)} copy(f32[2,3,3,1024]{3,0,2,1:T(2,128)} %param.15) | data formatting | bytes 147456 | tf_op args[5]
  4.3 128.8 %hyena_pair.1 = bf16[1024,2048]{1,0:T(8,128)(2,1)} custom-call(bf16[1024,2048]{1,0:T(8,128)(2,1)} %q1.1, bf16[1024,2048]{1,0:T(8,128)(2,1)} %k1.1, bf16[1024,2048]{1,0:T(8,128)(2,1)} %v1.1, bf16[1024,2048]{1,0:T(8,128)(2,1)} %k2.1, bf16[1024,2048]{1,0:T(8,128)(2,1)} %q2.1, f32[2,3,3,1024]{3,2,1,0:T(4,128)} %copy.11.cw, bf16[64,128]{1,0:T(8,128)(2,1)} %mr.1, ...), custom_call_target="tpu_custom_call" | custom-call | tf_op jit(solution)/shard_map/hyena_pair/pallas_call | solution.py:430
  133.2 4.8 %copy.15 = bf16[1024,2048]{1,0:T(8,128)(2,1)} copy(bf16[1024,2048]{1,0:T(8,128)(2,1)} %hyena_pair.1) | data formatting | bytes 8388608

commit v2 on v1

--- a/solution.py
+++ b/solution.py
@@ -34,7 +34,18 @@
 
 def short_filter(x, taps):
     w0, w1, w2 = taps
-    return w0 * x + w1 * pltpu.roll(x, 1, 1) + w2 * pltpu.roll(x, 2, 1)
+    back_one = pltpu.roll(x, 1, 1).astype(F32)
+    back_two = pltpu.roll(x, 2, 1).astype(F32)
+    return w0 * x.astype(F32) + w1 * back_one + w2 * back_two
+
+
+def grouped(start, stop, size, act):
+    def step(j, _):
+        for i in range(size):
+            act(start + j * size + i)
+        return _
+
+    lax.fori_loop(0, (stop - start) // size, step, 0)
 
 
 def to_rows(x, first, count, step, width):
@@ -46,7 +57,7 @@
 def kernel(
     n_ctx, n_mp, q1, k1, v1, k2, q2, cw, mr, rate, residue, gain, out,
     xin, hwide, hthin, wmed, wlong, readout, proj, ptwo, within, qnext, state, wcol,
-    pad, tapf, rate_t, res_t, fin, decay, got, carry, back, sums, sums_in,
+    pad, tapf, rate_t, res_t, fade, prod, mid, carried_in, fin, decay, got, carry, back, sums, sums_in,
     in_sem, hsend, hrecv, asend, arecv, bsend, brecv, msend, mrecv, osem,
 ):
     me = lax.axis_index("ctx")
@@ -114,16 +125,15 @@
         for stream in range(3):
             for tap in range(3):
                 at = layer * 9 + stream * 3 + tap
-                pad[at : at + 1, :] = cw[layer, stream, tap : tap + 1, :]
+                pad[at : at + 1, :] = cw[stream, tap, layer : layer + 1, :]
     pad[18:19, :] = gain[...]
     for t in range(tiles):
         wcol[t * LANES : (t + 1) * LANES, :] = pad[:, t * LANES : (t + 1) * LANES].T
     tapf[...] = mr[...].astype(F32)
-    pad[...] = jnp.zeros_like(pad)
-    pad[0:groups, 0:MODES] = rate[...]
-    rate_t[...] = pad[:, 0:LANES].T[0:MODES, :]
-    pad[0:groups, 0:MODES] = residue[...]
-    res_t[...] = pad[:, 0:LANES].T[0:MODES, :]
+    rate_t[...] = jnp.zeros_like(rate_t)
+    res_t[...] = jnp.zeros_like(res_t)
+    rate_t[:, 0:groups] = rate[...]
+    res_t[:, 0:groups] = residue[...]
 
     def mode_column(table, g):
         hit = lane_ids(MODES, LANES) == g
@@ -134,7 +144,7 @@
             jnp.broadcast_to(row, (LANES, LANES)), 0, 1, stride=1, stride_axis=0
         )
 
-    def tables(g, _):
+    def tables(g):
         above = lane_ids(LANES, LANES) >= lax.broadcasted_iota(jnp.int32, (LANES, LANES), 0)
         rate_c = mode_column(rate_t, g)
         amp = mode_column(res_t, g) * jnp.sqrt(rate_c)
@@ -155,10 +165,11 @@
         short = circulant(tapf[pl.ds(g, 1), :])
         wmed[g, 0:LANES, :] = jnp.where(above, 0.0, short).astype(BF16)
         wmed[g, LANES:, :] = jnp.where(above, short, 0.0).astype(BF16)
-        return _
+        block_at = lax.shift_right_logical(lane_ids(MODES, LANES), 4).astype(F32)
+        fade[g] = jnp.exp(-rate_c * (block_at * float(BLOCK)))
 
     early = groups // 2
-    lax.fori_loop(0, early, tables, 0)
+    grouped(0, early, 4, tables)
     pl.semaphore_wait(barrier, n_ctx - 1 + n_mp - 1)
 
     def start_halos(t, _):
@@ -173,9 +184,7 @@
         return _
 
     lax.fori_loop(0, tiles, start_late_halos, 0)
-    lax.fori_loop(early, groups, tables, 0)
-
-    keep = me > 0
+    grouped(early, groups, 4, tables)
 
     def columns(rows, layer, stream):
         at = layer * 9 + stream * 3
@@ -184,62 +193,76 @@
     def extended(s, rows):
         wide = s in (K1, V1)
         halo = hwide[s - K1, rows, :] if wide else hthin[{Q1: 0, K2: 1, Q2: 2}[s], rows, :]
-        halo = jnp.where(keep, halo.astype(F32), 0.0)
-        return jnp.concatenate([halo, xin[s, rows, :].astype(F32)], axis=1)
-
-    def produce(g, t, i):
-        rows = aligned(g, GROUP)
+        return jnp.concatenate([halo, xin[s, rows, :]], axis=1)
+
+    def make_product(t, i):
+        rows = aligned(t * per_tile + i, GROUP)
         key = short_filter(extended(K1, rows), columns(rows, 0, 1))
         value = short_filter(extended(V1, rows), columns(rows, 0, 2))
-        product = (key * value).astype(BF16)
+        prod[i] = (key * value).astype(BF16)
+
+    def make_layer(t, i):
+        g = t * per_tile + i
+        rows = aligned(g, GROUP)
         mixed = jnp.dot(
-            to_rows(product, 0, med_blocks + 1, TAPS, 2 * TAPS), wmed[g], preferred_element_type=F32
+            to_rows(prod[i], 0, med_blocks + 1, TAPS, 2 * TAPS), wmed[g], preferred_element_type=F32
         )
         mixed = jnp.concatenate(
             [mixed[j * GROUP : (j + 1) * GROUP, :] for j in range(med_blocks + 1)], axis=1
         )
         query = short_filter(extended(Q1, rows), columns(rows, 0, 0))
-        layer_one = (query * mixed).astype(BF16).astype(F32)
-        value_two = short_filter(layer_one, columns(rows, 1, 2))[:, LANES:]
+        mid[i] = (query * mixed).astype(BF16)
+
+    def make_second(t, i):
+        g = t * per_tile + i
+        rows = aligned(g, GROUP)
+        value_two = short_filter(mid[i], columns(rows, 1, 2))[:, LANES:]
         key_two = short_filter(extended(K2, rows), columns(rows, 1, 1))[:, LANES:]
         second = (key_two * value_two).astype(BF16)
-        pieces = to_rows(second, 0, blocks, BLOCK, BLOCK)
-        ptwo[g] = pieces
-        local = lax.dot_general(
-            proj[g], pieces, (((1,), (1,)), ((), ())), preferred_element_type=F32
-        )
-        rate_c = mode_column(rate_t, g)
+        ptwo[g] = to_rows(second, 0, blocks, BLOCK, BLOCK)
+
+    def make_states(t):
         lane = lane_ids(MODES, GROUP * blocks)
-        total = local
-        width = 1
-        while width < blocks:
-            moved = pltpu.roll(total, width * GROUP, 1)
-            factor = jnp.exp(-rate_c * float(BLOCK * width))
-            total = total + jnp.where(lane >= width * GROUP, factor * moved, 0.0)
-            width *= 2
-        state[g] = jnp.where(lane >= GROUP, pltpu.roll(total, GROUP, 1), 0.0)
-        spot = lax.shift_right_logical(lane, 4) == i
-        moved = pltpu.roll(total, lax.rem(i * GROUP + GROUP, LANES), 1)
-        drop = jnp.exp(-rate_c * float(length))
+        ends = jnp.zeros((MODES, LANES), F32)
+        drops = jnp.zeros((MODES, LANES), F32)
+        for i in range(per_tile):
+            g = t * per_tile + i
+            total = lax.dot_general(
+                proj[g], ptwo[g], (((1,), (1,)), ((), ())), preferred_element_type=F32
+            )
+            rate_c = mode_column(rate_t, g)
+            width = 1
+            while width < blocks:
+                moved = pltpu.roll(total, width * GROUP, 1)
+                factor = jnp.exp(-rate_c * float(BLOCK * width))
+                total = total + jnp.where(lane >= width * GROUP, factor * moved, 0.0)
+                width *= 2
+            state[g] = jnp.where(lane >= GROUP, pltpu.roll(total, GROUP, 1), 0.0)
+            spot = lax.shift_right_logical(lane, 4) == i
+            moved = pltpu.roll(total, (i + 1) * GROUP % LANES, 1) if i + 1 < blocks else total
+            ends = jnp.where(spot, moved, ends)
+            drops = jnp.where(spot, jnp.exp(-rate_c * float(length)), drops)
         for c in range(cuts):
             part = slice(c * share, (c + 1) * share)
-            at = t * cuts + c
-            fin[at] = jnp.where(spot[part], moved[part], fin[at])
-            decay[at] = jnp.where(spot[part], jnp.broadcast_to(drop, moved.shape)[part], decay[at])
-
-    fin[...] = jnp.zeros_like(fin)
-    decay[...] = jnp.zeros_like(decay)
+            fin[t * cuts + c] = ends[part]
+            decay[t * cuts + c] = drops[part]
 
     def tile_step(t, _):
         for s in first_four:
             load_copy(s, t).wait()
             halo_copy(s, t).wait_recv()
 
-        def group_step(i, _):
-            produce(t * per_tile + i, t, i)
-            return _
-
-        return lax.fori_loop(0, per_tile, group_step, _)
+        @pl.when(me == 0)
+        def clear():
+            rows = aligned(t, LANES)
+            hwide[:, rows, :] = jnp.zeros((2, LANES, 2 * LANES), BF16)
+            hthin[0:2, rows, :] = jnp.zeros((2, LANES, LANES), BF16)
+
+        grouped(0, per_tile, 1, functools.partial(make_product, t))
+        grouped(0, per_tile, 2, functools.partial(make_layer, t))
+        grouped(0, per_tile, 1, functools.partial(make_second, t))
+        make_states(t)
+        return _
 
     lax.fori_loop(0, tiles, tile_step, 0)
 
@@ -297,15 +320,19 @@
         load_copy(Q2, t).wait()
         halo_copy(Q2, t).wait_recv()
 
-        def group_step(i, _):
+        @pl.when(me == 0)
+        def clear():
+            hthin[2, aligned(t, LANES), :] = jnp.zeros((LANES, LANES), BF16)
+
+        def inner_group(i):
             g = t * per_tile + i
             rows = aligned(g, GROUP)
             within[g] = jnp.dot(ptwo[g], wlong[g], preferred_element_type=F32)
             query = short_filter(extended(Q2, rows), columns(rows, 1, 0))[:, LANES:]
             qnext[g] = to_rows(query, 0, blocks, BLOCK, BLOCK)
-            return _
-
-        return lax.fori_loop(0, per_tile, group_step, _)
+
+        grouped(0, per_tile, 2, inner_group)
+        return _
 
     half = (tiles + 1) // 2
     lax.fori_loop(0, half, inner_part, 0)
@@ -325,25 +352,19 @@
 
     def finish_tile(t, _):
         incoming = jnp.concatenate([back[t * cuts + c] for c in range(cuts)], axis=0)
-
-        def group_step(i, _):
+        turned = [incoming] + [pltpu.roll(incoming, k * GROUP, 1) for k in range(1, blocks)]
+        block_at = lax.shift_right_logical(lane_ids(MODES, LANES), 4)
+        for i in range(per_tile):
             g = t * per_tile + i
-            lane = lane_ids(MODES, LANES)
-            seed = jnp.where(
-                lane < GROUP, pltpu.roll(incoming, lax.rem(LANES - i * GROUP, LANES), 1), 0.0
-            )
-            width = 1
-            while width < blocks:
-                seed = seed + pltpu.roll(seed, width * GROUP, 1)
-                width *= 2
-            rate_c = mode_column(rate_t, g)
-            block_at = lax.shift_right_logical(lane, 4).astype(F32)
-            total = state[g] + seed * jnp.exp(-rate_c * (block_at * float(BLOCK)))
-            high, low = split_pair(total)
-            stacked = jnp.concatenate([high, high, low], axis=0)
-            carried = lax.dot_general(
-                stacked, readout[g], (((0,), (0,)), ((), ())), preferred_element_type=F32
-            )
+            seed = turned[-i % blocks]
+            for b in range(1, blocks):
+                seed = jnp.where(block_at == b, turned[(b - i) % blocks], seed)
+            high, low = split_pair(state[g] + seed * fade[g])
+            carried_in[i] = jnp.concatenate([high, high, low], axis=0).T
+
+        def finish_group(i):
+            g = t * per_tile + i
+            carried = jnp.dot(carried_in[i], readout[g], preferred_element_type=F32)
             long_two = (within[g] + carried).astype(BF16).astype(F32)
             gated = qnext[g] * long_two
             within[g] = gated
@@ -351,9 +372,9 @@
             for b in range(blocks):
                 low_rows = square[b * GROUP : b * GROUP + 8, :]
                 sums[b] = sums[b] + (low_rows + square[b * GROUP + 8 : (b + 1) * GROUP, :])
-            return _
-
-        return lax.fori_loop(0, per_tile, group_step, _)
+
+        grouped(0, per_tile, 2, finish_group)
+        return _
 
     lax.fori_loop(0, tiles, finish_tile, 0)
 
@@ -449,6 +470,10 @@
             pltpu.VMEM((groups, TAPS), F32),
             pltpu.VMEM((MODES, LANES), F32),
             pltpu.VMEM((MODES, LANES), F32),
+            pltpu.VMEM((groups, MODES, LANES), F32),
+            pltpu.VMEM((LANES // GROUP, GROUP, length + 2 * LANES), BF16),
+            pltpu.VMEM((LANES // GROUP, GROUP, length + LANES), BF16),
+            pltpu.VMEM((LANES // GROUP, GROUP * blocks, 3 * MODES), BF16),
             message,
             message,
             message,
@@ -473,7 +498,8 @@
         name="hyena_pair",
     )(
         query_one, key_one, value_one, key_two, query_two,
-        conv_weights, mr_filter, li_rate, li_residue, norm_gain.reshape(1, chans),
+        jnp.transpose(conv_weights, (1, 2, 0, 3)), mr_filter, li_rate.T, li_residue.T,
+        norm_gain.reshape(1, chans),
     )
 
 

time: 138 us -> 90.2 us (0.65)
  Pallas kernels: 129 us -> 85.1 us
  local copies, waits for them, and re-layouts: 9.12 us -> 4.79 us
    pallas_call x1, Pallas kernels: 129 us -> 85.1 us  [per_device(): pl.pallas_call(functools.partial(kernel, n_ctx, n_mp), out_shape=jax.Shap...]
    unnamed x4 -> x1, local copies, waits for them, and re-layouts: 9.12 us -> 4.79 us
where the time goes in v2:
time: 90.2 us; the launch traced here: 89.9 us
  Pallas kernels  85.1 us (94%)
  local copies, waits for them, and re-layouts  4.79 us (5%)
    pallas_call x1, Pallas kernels, per_device(): pl.pallas_call(functools.partial(kernel, n_ctx, n_mp), out_shape=jax.Shap...  85.1 us
    unnamed x1, local copies, waits for them, and re-layouts  4.79 us

profile of v2, /device:TPU:0, one launch (start us, length us, event | category | flops | bytes accessed | tf_op | source)
XLA Modules:
  0.0 89.9 jit_solution(8925712793231240236)
XLA Ops:
  0.0 85.1 %hyena_pair.1 = bf16[1024,2048]{1,0:T(8,128)(2,1)} custom-call(bf16[1024,2048]{1,0:T(8,128)(2,1)} %q1.1, bf16[1024,2048]{1,0:T(8,128)(2,1)} %k1.1, bf16[1024,2048]{1,0:T(8,128)(2,1)} %v1.1, bf16[1024,2048]{1,0:T(8,128)(2,1)} %k2.1, bf16[1024,2048]{1,0:T(8,128)(2,1)} %q2.1, f32[3,3,2,1024]{3,2,1,0:T(2,128)} %bitcast.4, bf16[64,128]{1,0:T(8,128)(2,1)} %mr.1, ...), custom_call_target="tpu_custom_call" | custom-call | tf_op jit(solution)/shard_map/hyena_pair/pallas_call | solution.py:451
  85.1 4.8 %copy.12 = bf16[1024,2048]{1,0:T(8,128)(2,1)} copy(bf16[1024,2048]{1,0:T(8,128)(2,1)} %hyena_pair.1) | data formatting | bytes 8388608

commit v3 on v2

--- a/solution.py
+++ b/solution.py
@@ -13,6 +13,8 @@
 MODES = 16
 LANES = 128
 MESH = pl.DeviceIdType.MESH
+FIRST_LIMIT = 54 * 2**20
+SECOND_LIMIT = 16 * 2**20
 F32 = jnp.float32
 BF16 = jnp.bfloat16
 Q1, K1, V1, K2, Q2 = range(5)
@@ -55,10 +57,10 @@
 
 
 def kernel(
-    n_ctx, n_mp, q1, k1, v1, k2, q2, cw, mr, rate, residue, gain, out,
-    xin, hwide, hthin, wmed, wlong, readout, proj, ptwo, within, qnext, state, wcol,
+    n_ctx, n_mp, q1, k1, v1, k2, q2, cw, mr, rate, residue, gain,
+    within, scale_out, xin, hwide, hthin, wmed, wlong, readout, proj, ptwo, qnext, state, wcol,
     pad, tapf, rate_t, res_t, fade, prod, mid, carried_in, fin, decay, got, carry, back, sums, sums_in,
-    in_sem, hsend, hrecv, asend, arecv, bsend, brecv, msend, mrecv, osem,
+    in_sem, hsend, hrecv, asend, arecv, bsend, brecv, msend, mrecv,
 ):
     me = lax.axis_index("ctx")
     my_mp = lax.axis_index("mp")
@@ -169,7 +171,7 @@
         fade[g] = jnp.exp(-rate_c * (block_at * float(BLOCK)))
 
     early = groups // 2
-    grouped(0, early, 4, tables)
+    grouped(0, early, 2, tables)
     pl.semaphore_wait(barrier, n_ctx - 1 + n_mp - 1)
 
     def start_halos(t, _):
@@ -184,7 +186,7 @@
         return _
 
     lax.fori_loop(0, tiles, start_late_halos, 0)
-    grouped(early, groups, 4, tables)
+    grouped(early, groups, 2, tables)
 
     def columns(rows, layer, stream):
         at = layer * 9 + stream * 3
@@ -258,9 +260,9 @@
             hwide[:, rows, :] = jnp.zeros((2, LANES, 2 * LANES), BF16)
             hthin[0:2, rows, :] = jnp.zeros((2, LANES, LANES), BF16)
 
-        grouped(0, per_tile, 1, functools.partial(make_product, t))
-        grouped(0, per_tile, 2, functools.partial(make_layer, t))
-        grouped(0, per_tile, 1, functools.partial(make_second, t))
+        grouped(0, per_tile, 4, functools.partial(make_product, t))
+        grouped(0, per_tile, 4, functools.partial(make_layer, t))
+        grouped(0, per_tile, 4, functools.partial(make_second, t))
         make_states(t)
         return _
 
@@ -331,7 +333,7 @@
             query = short_filter(extended(Q2, rows), columns(rows, 1, 0))[:, LANES:]
             qnext[g] = to_rows(query, 0, blocks, BLOCK, BLOCK)
 
-        grouped(0, per_tile, 2, inner_group)
+        grouped(0, per_tile, 4, inner_group)
         return _
 
     half = (tiles + 1) // 2
@@ -362,18 +364,22 @@
             high, low = split_pair(state[g] + seed * fade[g])
             carried_in[i] = jnp.concatenate([high, high, low], axis=0).T
 
+        def gain_rows(g):
+            gain_c = wcol[aligned(g, GROUP), 18:19]
+            return jnp.concatenate([gain_c] * blocks, axis=0)
+
         def finish_group(i):
             g = t * per_tile + i
             carried = jnp.dot(carried_in[i], readout[g], preferred_element_type=F32)
             long_two = (within[g] + carried).astype(BF16).astype(F32)
             gated = qnext[g] * long_two
-            within[g] = gated
+            within[g] = gated * gain_rows(g)
             square = gated * gated
             for b in range(blocks):
                 low_rows = square[b * GROUP : b * GROUP + 8, :]
                 sums[b] = sums[b] + (low_rows + square[b * GROUP + 8 : (b + 1) * GROUP, :])
 
-        grouped(0, per_tile, 2, finish_group)
+        grouped(0, per_tile, 4, finish_group)
         return _
 
     lax.fori_loop(0, tiles, finish_tile, 0)
@@ -398,30 +404,7 @@
     whole = sums_in[0]
     for i in range(1, n_mp):
         whole = whole + sums_in[i]
-    scale = lax.rsqrt(whole / float(n_mp * chans) + 1e-05)
-    sums[...] = jnp.broadcast_to(scale[:, None, :], sums.shape)
-
-    def out_copy(t):
-        rows = aligned(t, LANES)
-        return pltpu.make_async_copy(xin.at[Q1, rows, :], out.at[rows, :], osem.at[t])
-
-    def scale_tile(t, _):
-        def group_step(i, _):
-            g = t * per_tile + i
-            rows = aligned(g, GROUP)
-            gain_c = wcol[rows, 18:19]
-            gated = within[g]
-            for b in range(blocks):
-                scale_b = jnp.concatenate([sums[b], sums[b]], axis=0)
-                piece = gated[b * GROUP : (b + 1) * GROUP, :] * scale_b * gain_c
-                xin[Q1, rows, b * BLOCK : (b + 1) * BLOCK] = piece.astype(BF16)
-            return _
-
-        lax.fori_loop(0, per_tile, group_step, 0)
-        out_copy(t).start()
-        return _
-
-    lax.fori_loop(0, tiles, scale_tile, 0)
+    scale_out[...] = lax.rsqrt(whole / float(n_mp * chans) + 1e-05)
 
     for peer in mp_peers:
         sum_copy(peer, my_mp).wait_send()
@@ -431,8 +414,39 @@
     def drain(t, _):
         for s in range(5):
             halo_copy(s, t).wait_send()
+        return _
+
+    lax.fori_loop(0, tiles, drain, 0)
+
+
+def scale_kernel(weighted, scale, out, made, osem):
+    groups, _, block = weighted.shape
+    blocks = scale.shape[0]
+    per_tile = LANES // GROUP
+
+    def out_copy(t):
+        rows = aligned(t, LANES)
+        return pltpu.make_async_copy(made.at[rows, :], out.at[rows, :], osem.at[t])
+
+    tiles = groups // per_tile
+
+    def scale_tile(t, carry):
+        def scale_group(i):
+            g = t * per_tile + i
+            rows = aligned(g, GROUP)
+            for b in range(blocks):
+                piece = weighted[g, b * GROUP : (b + 1) * GROUP, :] * scale[b : b + 1, :]
+                made[rows, b * block : (b + 1) * block] = piece.astype(BF16)
+
+        grouped(0, per_tile, 4, scale_group)
+        out_copy(t).start()
+        return carry
+
+    lax.fori_loop(0, tiles, scale_tile, 0)
+
+    def drain(t, carry):
         out_copy(t).wait()
-        return _
+        return carry
 
     lax.fori_loop(0, tiles, drain, 0)
 
@@ -448,11 +462,11 @@
     vmem_spec = pl.BlockSpec(memory_space=pltpu.VMEM)
     dma = pltpu.SemaphoreType.DMA
     message = pltpu.VMEM((n_ctx, share, LANES), F32)
-    return pl.pallas_call(
+    weighted, scale = pl.pallas_call(
         functools.partial(kernel, n_ctx, n_mp),
-        out_shape=jax.ShapeDtypeStruct((chans, length), BF16),
+        out_shape=(pltpu.VMEM((groups, GROUP * blocks, BLOCK), F32), pltpu.VMEM((blocks, BLOCK), F32)),
         in_specs=[any_spec] * 5 + [vmem_spec] * 5,
-        out_specs=any_spec,
+        out_specs=(vmem_spec, vmem_spec),
         scratch_shapes=[
             pltpu.VMEM((5, chans, length), BF16),
             pltpu.VMEM((2, chans, 2 * LANES), BF16),
@@ -462,7 +476,6 @@
             pltpu.VMEM((groups, 3 * MODES, BLOCK), BF16),
             pltpu.VMEM((groups, MODES, BLOCK), BF16),
             pltpu.VMEM((groups, GROUP * blocks, BLOCK), BF16),
-            pltpu.VMEM((groups, GROUP * blocks, BLOCK), F32),
             pltpu.VMEM((groups, GROUP * blocks, BLOCK), F32),
             pltpu.VMEM((groups, MODES, LANES), F32),
             pltpu.VMEM((chans, LANES), F32),
@@ -490,10 +503,9 @@
             dma((n_ctx,)),
             dma((n_mp,)),
             dma((n_mp,)),
-            dma((tiles,)),
         ],
         compiler_params=pltpu.CompilerParams(
-            collective_id=0, has_side_effects=True, vmem_limit_bytes=67043328
+            collective_id=0, has_side_effects=True, vmem_limit_bytes=FIRST_LIMIT
         ),
         name="hyena_pair",
     )(
@@ -501,6 +513,15 @@
         jnp.transpose(conv_weights, (1, 2, 0, 3)), mr_filter, li_rate.T, li_residue.T,
         norm_gain.reshape(1, chans),
     )
+    return pl.pallas_call(
+        scale_kernel,
+        out_shape=jax.ShapeDtypeStruct((chans, length), BF16),
+        in_specs=[vmem_spec, vmem_spec],
+        out_specs=any_spec,
+        scratch_shapes=[pltpu.VMEM((chans, length), BF16), dma((tiles,))],
+        compiler_params=pltpu.CompilerParams(vmem_limit_bytes=SECOND_LIMIT),
+        name="scale_rows",
+    )(weighted, scale)
 
 
 def solution(mesh):

time: 90.2 us -> 72.4 us (0.80)
  Pallas kernels: 85.1 us -> 72.1 us
  local copies, waits for them, and re-layouts: 4.79 us -> 0 us
    pallas_call x1 -> x2, Pallas kernels: 85.1 us -> 72.1 us  [the longest x1 69.9 us: per_device(): pl.pallas_call(functools.partial(kernel, n_ctx, n_mp), out_shape=(pltpu.V...]
    unnamed x1 -> x0, local copies, waits for them, and re-layouts: 4.79 us -> none
where the time goes in v3:
time: 72.4 us; the launch traced here: 72.1 us
  Pallas kernels  72.1 us (100%)
    pallas_call x1, Pallas kernels, per_device(): pl.pallas_call(functools.partial(kernel, n_ctx, n_mp), out_shape=(pltpu.V...  69.9 us
    pallas_call x1, Pallas kernels, per_device(): pl.pallas_call(scale_kernel, out_shape=jax.ShapeDtypeStruct((chans, lengt...  2.14 us

profile of v3, /device:TPU:0, one launch (start us, length us, event | category | flops | bytes accessed | tf_op | source)
XLA Modules:
  0.0 72.1 jit_solution(5653176940990179177)
XLA Ops:
  0.0 69.9 %hyena_pair.1 = (f32[64,128,256]{2,1,0:T(8,128)S(1)}, f32[8,256]{1,0:T(8,128)S(1)}) custom-call(bf16[1024,2048]{1,0:T(8,128)(2,1)} %q1.1, bf16[1024,2048]{1,0:T(8,128)(2,1)} %k1.1, bf16[1024,2048]{1,0:T(8,128)(2,1)} %v1.1, bf16[1024,2048]{1,0:T(8,128)(2,1)} %k2.1, bf16[1024,2048]{1,0:T(8,128)(2,1)} %q2.1, f32[3,3,2,1024]{3,2,1,0:T(2,128)} %bitcast.4, ...), custom_call_target="tpu_custom_call" | custom-call | tf_op jit(solution)/shard_map/hyena_pair/pallas_call | solution.py:465
  69.9 2.1 %scale_rows.1 = bf16[1024,2048]{1,0:T(8,128)(2,1)} custom-call(f32[64,128,256]{2,1,0:T(8,128)S(1)} %get-tuple-element.7.weighted, f32[8,256]{1,0:T(8,128)S(1)} %get-tuple-element.8.scale), custom_call_target="tpu_custom_call" | custom-call | tf_op jit(solution)/shard_map/scale_rows/pallas_call | solution.py:516
